TPU v7x, 256 devices: a whole 4x4x8 slice. The times are simulated.
256 devices in a mesh: gx: 16 (over z_lo, x, core), gy: 4 (over y), tx: 4 (over z_hi).
Axes of the slice: x: 4, y: 4, z: 8 (z_hi: 4, z_lo: 2; z = z_hi * 2 + z_lo), core: 2. Of those that a mesh axis runs over, the one named last changes fastest.
Arguments:
- src_cell: int32 [8], P('tx'), may hold values from 0 to 524287
- basis: bfloat16 [16, 2, 3, 8, 128, 512], P('tx', None, None, None, 'gx', 'gy'), as said below
- images: bfloat16 [16, 2, 3, 8, 128, 512], P('tx', None, None, None, 'gx', 'gy'), as said below
- induction: bfloat16 [3, 8, 128, 512], P(None, 'tx', 'gx', 'gy'), may hold values from 0.25 to 4
Outputs:
- solution: float32 [8, 2, 3, 8, 128, 512], P('tx', None, None, None, 'gx', 'gy')
- residual: float32 [8, 2, 3, 8, 128, 512], P('tx', None, None, None, 'gx', 'gy')
Inputs may be any that keep to these rules, and one draw needn't show every extreme that they name: `basis`: entries of order one. `images`: entries of order one.
All inputs are finite; a program needn't handle non-finite values.
Results may differ from a plain program's by a relative error of at most 0.0003.
Values may be sent and summed in bfloat16 or wider, within the bound.
No kernel may reach another device: no remote copies, remote signals or barrier semaphores. Data moves between devices by JAX's collectives and lax.ppermute only.
A program may use at most 64 MiB of HBM per device.

v0:
```python
import jax
import jax.numpy as jnp
from jax import lax
from jax.sharding import PartitionSpec as P

CYCLES = 2
ARNOLDI = 2
eps = 1e-06


def with_halo(x, sides, width):
    for axis, dim in sides:
        size, length = (lax.axis_size(axis), x.shape[dim])
        up = [(i, (i + 1) % size) for i in range(size - 1)]
        down = [(j, i) for i, j in up]
        last = lax.slice_in_dim(x, length - width, length, axis=dim)
        initial = lax.slice_in_dim(x, 0, width, axis=dim)
        before = lax.ppermute(last, axis, up)
        after = lax.ppermute(initial, axis, down)
        x = jnp.concatenate([before, x, after], axis=dim)
    return x


def differ(field, axis, forward):
    axis = field.ndim + axis
    count = field.shape[axis]
    delta = lax.slice_in_dim(field, 1, count, axis=axis) - lax.slice_in_dim(
        field, 0, count - 1, axis=axis
    )
    zero = jnp.zeros_like(lax.slice_in_dim(field, 0, 1, axis=axis))
    if forward:
        return jnp.concatenate([delta, zero], axis=axis)
    return jnp.concatenate([zero, delta], axis=axis)


def curl_curl(padded):
    e_x = padded[..., 0, :, :, :]
    e_y = padded[..., 1, :, :, :]
    e_z = padded[..., 2, :, :, :]
    b_x = differ(e_z, -1, True) - differ(e_y, -3, True)
    b_y = differ(e_x, -3, True) - differ(e_z, -2, True)
    b_z = differ(e_y, -2, True) - differ(e_x, -1, True)
    c_x = differ(b_z, -1, False) - differ(b_y, -3, False)
    c_y = differ(b_x, -3, False) - differ(b_z, -2, False)
    c_z = differ(b_y, -2, False) - differ(b_x, -1, False)
    whole = jnp.stack([c_x, c_y, c_z], axis=-4)
    return whole[..., 1:-1, 1:-1, 1:-1]


def apply_operator(field, induct):
    framed = with_halo(field, (("gx", 4), ("gy", 5)), 1)
    padded = jnp.pad(framed, [(0, 0), (0, 0), (0, 0), (1, 1), (0, 0), (0, 0)])
    curled = curl_curl(padded)
    real_part = curled[:, 0] - induct[None] * field[:, 1]
    imag_part = curled[:, 1] + induct[None] * field[:, 0]
    return jnp.stack([real_part, imag_part], axis=1)


def source_field(cells, z_pos, x_pos, y_pos, size_x, size_y, induct):
    plane = size_x * size_y
    src_z = cells // plane
    rest = cells % plane
    src_x = rest // size_y
    src_y = rest % size_y
    d_z = (z_pos[None, :] - src_z[:, None]).astype(jnp.float32)
    d_x = (x_pos[None, :] - src_x[:, None]).astype(jnp.float32)
    d_y = (y_pos[None, :] - src_y[:, None]).astype(jnp.float32)
    dist = jnp.sqrt(
        d_z[:, :, None, None] ** 2 + d_x[:, None, :, None] ** 2 + d_y[:, None, None, :] ** 2
    )
    primary = jnp.exp(-dist / ((size_x + size_y) / 8.0))
    weights = jnp.array([1.0, 0.5, 0.25], dtype=jnp.float32)
    real_part = (induct - 1.0)[None] * weights[None, :, None, None, None] * primary[:, None]
    return jnp.stack([real_part, 0.5 * real_part], axis=1)


def inner_basis(vectors, field):
    return jnp.einsum(
        "kpczxy,spczxy->ks",
        vectors,
        field,
        precision=lax.Precision.HIGHEST,
        preferred_element_type=jnp.float32,
    )


def combine(coeffs, vectors):
    return jnp.einsum(
        "ks,kpczxy->spczxy",
        coeffs,
        vectors,
        precision=lax.Precision.HIGHEST,
        preferred_element_type=jnp.float32,
    )


def per_source(left, right):
    return jnp.sum(left * right, axis=(1, 2, 3, 4, 5))


def expand(values):
    return values[:, None, None, None, None, None]


def small_solve(matrix, rhs):
    factor = jnp.linalg.cholesky(matrix)
    return jax.scipy.linalg.cho_solve((factor, True), rhs)


def on_device(src_cell, basis, images, induction):
    all_basis, all_images, gathered = (
        lax.all_gather(basis, "tx", axis=0, tiled=True),
        lax.all_gather(images, "tx", axis=0, tiled=True),
        lax.all_gather(induction, "tx", axis=1, tiled=True),
    )
    induct = gathered.astype(jnp.float32)
    depth = basis.shape[3]
    width_x = basis.shape[4]
    width_y = basis.shape[5]
    size_x = width_x * lax.axis_size("gx")
    size_y = width_y * lax.axis_size("gy")
    z_pos = jnp.arange(depth, dtype=jnp.int32)
    x_pos = lax.axis_index("gx") * width_x + jnp.arange(width_x, dtype=jnp.int32)
    y_pos = lax.axis_index("gy") * width_y + jnp.arange(width_y, dtype=jnp.int32)
    rhs = source_field(src_cell, z_pos, x_pos, y_pos, size_x, size_y, induct)
    gram_part = jnp.einsum(
        "kpczxy,lpczxy->kl", all_images, all_images, preferred_element_type=jnp.float32
    )
    gram, start_inner = lax.psum((gram_part, inner_basis(all_images, rhs)), ("gx", "gy"))
    factor = jnp.linalg.cholesky(gram)
    h_zero = jax.scipy.linalg.cho_solve((factor, True), start_inner)
    residual = rhs - combine(h_zero, all_images)
    solution = combine(h_zero, all_basis)
    for cycle in range(CYCLES):
        beta = jnp.sqrt(lax.psum(per_source(residual, residual), ("gx", "gy")) + eps)
        krylov = [residual / expand(beta)]
        h_cols = []
        g_cols = []
        for step in range(ARNOLDI):
            work = apply_operator(krylov[step], induct)
            g_raw = lax.psum(inner_basis(all_images, work), ("gx", "gy"))
            g_now = jax.scipy.linalg.cho_solve((factor, True), g_raw)
            work = work - combine(g_now, all_images)
            h_now = lax.psum(jnp.stack([per_source(vec, work) for vec in krylov]), ("gx", "gy"))
            for index in range(step + 1):
                work = work - expand(h_now[index]) * krylov[index]
            h_next = jnp.sqrt(lax.psum(per_source(work, work), ("gx", "gy")) + eps)
            krylov.append(work / expand(h_next))
            pad_rows = jnp.zeros((ARNOLDI - step - 1, h_next.shape[0]), dtype=jnp.float32)
            h_cols.append(jnp.concatenate([h_now, h_next[None], pad_rows], axis=0))
            g_cols.append(g_now)
        hess = jnp.stack(h_cols, axis=1)
        g_all = jnp.stack(g_cols, axis=1)
        normal = jnp.einsum("ijs,iks->sjk", hess, hess, precision=lax.Precision.HIGHEST)
        target = beta[:, None] * jnp.transpose(hess[0])
        y_coef = jax.vmap(small_solve)(normal, target)
        update = expand(y_coef[:, 0]) * krylov[0]
        step = 1
        update = update + expand(y_coef[:, step]) * krylov[step]
        u_coef = jnp.einsum("kjs,sj->ks", g_all, y_coef, precision=lax.Precision.HIGHEST)
        solution = solution + update - combine(u_coef, all_basis)
        first = jnp.zeros((ARNOLDI + 1, beta.shape[0]), dtype=jnp.float32).at[0].set(beta)
        t_coef = first - jnp.einsum("ijs,sj->is", hess, y_coef, precision=lax.Precision.HIGHEST)
        residual = expand(t_coef[0]) * krylov[0]
        for index in range(1, ARNOLDI + 1):
            residual = residual + expand(t_coef[index]) * krylov[index]
    return (solution, residual)


def solution(mesh):
    in_specs = (
        P("tx"),
        P("tx", None, None, None, "gx", "gy"),
        P("tx", None, None, None, "gx", "gy"),
        P(None, "tx", "gx", "gy"),
    )
    out_specs = (P("tx", None, None, None, "gx", "gy"), P("tx", None, None, None, "gx", "gy"))
    return jax.shard_map(
        on_device, mesh=mesh, in_specs=in_specs, out_specs=out_specs, check_vma=False
    )
```

profile of v0, /device:TPU:40, one launch (start us, length us, event | category | flops | bytes accessed | tf_op | source)
XLA Modules:
  0.0 2366.0 jit_solution(5453150176349590648)
XLA Ops:
  7.9 16.6 all_gather.10
  26.5 26.6 %all-gather.3.cloned.1.call-done = bf16[16,2,3,8,8,128]{5,4,3,2,1,0:T(8,128)(2,1)} async-done(((bf16[4,2,3,8,8,128]{5,4,3,2,1,0:T(8,128)(2,1)}), bf16[16,2,3,8,8,128]{5,4,3,2,1,0:T(8,128)(2,1)}) %all-gather.3.cloned.1.call-update) | async-done | bytes 1572880 | tf_op jit(solution)/shard_map/all_gather | solution.py:113
  53.1 5.4 convolution_bitcast_fusion
  58.5 3.7 convolution_bitcast_fusion.8
  62.2 144.3 %all-reduce.54 = (f32[16,2]{0,1:T(2,128)S(1)}, f32[16,16]{0,1:T(8,128)S(1)}) all-reduce(f32[16,2]{0,1:T(2,128)S(1)} %convolution_bitcast_fusion.8, f32[16,16]{0,1:T(8,128)S(1)} %convolution_bitcast_fusion), channel_id=1, replica_groups=mesh['gx'=16,'gy'=4,'tx'=4] {'gx','gy'}, use_global_device_ids=true, to_apply=%region_3.4 | all-reduce | flops 288 | bytes 2304 | tf_op jit(solution)/shard_map/psum | solution.py:129
  210.9 3.3 multiply_reduce_fusion.11
  214.2 143.8 %psum.114 = f32[2]{0:T(128)S(1)} all-reduce(f32[2]{0:T(128)S(1)} %get-tuple-element.119), channel_id=1, replica_groups=mesh['gx'=16,'gy'=4,'tx'=4] {'gx','gy'}, use_global_device_ids=true, to_apply=%region_5.7 | all-reduce | flops 2 | bytes 16 | tf_op jit(solution)/shard_map/psum | solution.py:135
  360.2 5.8 collective-permute-start.1
  370.4 4.1 collective-permute-start.3
  374.6 4.7 collective-permute-done.2
  379.3 1.9 collective-permute-done.3
  381.2 2.4 select_maximum_fusion.12
  391.2 3.7 convolution_bitcast_fusion.7
  394.9 140.9 %psum.115 = f32[16,2]{0,1:T(2,128)S(1)} all-reduce(f32[16,2]{0,1:T(2,128)S(1)} %convolution_bitcast_fusion.7), channel_id=1, replica_groups=mesh['gx'=16,'gy'=4,'tx'=4] {'gx','gy'}, use_global_device_ids=true, to_apply=%region_6.8 | all-reduce | flops 32 | bytes 256 | tf_op jit(solution)/shard_map/psum | solution.py:141
  536.1 3.3 multiply_reduce_fusion.10
  539.4 139.6 %psum.116 = f32[1,2]{1,0:T(1,128)S(1)} all-reduce(f32[1,2]{1,0:T(1,128)S(1)} %bitcast.337), channel_id=1, replica_groups=mesh['gx'=16,'gy'=4,'tx'=4] {'gx','gy'}, use_global_device_ids=true, to_apply=%region_8.10 | all-reduce | flops 2 | bytes 16 | tf_op jit(solution)/shard_map/psum | solution.py:144
  679.7 139.5 %psum.117 = f32[2]{0:T(128)S(1)} all-reduce(f32[2]{0:T(128)S(1)} %get-tuple-element.49), channel_id=1, replica_groups=mesh['gx'=16,'gy'=4,'tx'=4] {'gx','gy'}, use_global_device_ids=true, to_apply=%region_10.12 | all-reduce | flops 2 | bytes 16 | tf_op jit(solution)/shard_map/psum | solution.py:147
  821.4 5.8 collective-permute-start.5
  831.6 3.9 collective-permute-start.7
  835.6 4.9 collective-permute-done.6
  840.5 1.9 collective-permute-done.7
  842.4 2.4 select_maximum_fusion.8
  852.5 3.6 convolution_bitcast_fusion.6
  856.1 141.1 %psum.118 = f32[16,2]{0,1:T(2,128)S(1)} all-reduce(f32[16,2]{0,1:T(2,128)S(1)} %convolution_bitcast_fusion.6), channel_id=1, replica_groups=mesh['gx'=16,'gy'=4,'tx'=4] {'gx','gy'}, use_global_device_ids=true, to_apply=%region_11.13 | all-reduce | flops 32 | bytes 256 | tf_op jit(solution)/shard_map/psum | solution.py:141
  997.4 3.4 multiply_reduce_fusion.8
  1000.9 139.0 %psum.119 = f32[2,2]{1,0:T(2,128)S(1)} all-reduce(f32[2,2]{1,0:T(2,128)S(1)} %pad_maximum_fusion.26), channel_id=1, replica_groups=mesh['gx'=16,'gy'=4,'tx'=4] {'gx','gy'}, use_global_device_ids=true, to_apply=%region_14.16 | all-reduce | flops 4 | bytes 32 | tf_op jit(solution)/shard_map/psum | solution.py:144
  1140.6 140.2 %psum.120 = f32[2]{0:T(128)S(1)} all-reduce(f32[2]{0:T(128)S(1)} %get-tuple-element.47), channel_id=1, replica_groups=mesh['gx'=16,'gy'=4,'tx'=4] {'gx','gy'}, use_global_device_ids=true, to_apply=%region_16.18 | all-reduce | flops 2 | bytes 16 | tf_op jit(solution)/shard_map/psum | solution.py:147
  1283.8 139.0 %psum.121 = f32[2]{0:T(128)S(1)} all-reduce(f32[2]{0:T(128)S(1)} %get-tuple-element.45), channel_id=1, replica_groups=mesh['gx'=16,'gy'=4,'tx'=4] {'gx','gy'}, use_global_device_ids=true, to_apply=%region_20.24 | all-reduce | flops 2 | bytes 16 | tf_op jit(solution)/shard_map/psum | solution.py:135
  1425.0 5.8 collective-permute-start.9
  1430.8 3.7 convolution_add_fusion
  1437.3 4.1 collective-permute-start.11
  1441.5 5.5 collective-permute-done.10
  1449.0 2.4 select_maximum_fusion.4
  1459.0 3.7 convolution_bitcast_fusion.5
  1462.7 140.7 %psum.122 = f32[16,2]{0,1:T(2,128)S(1)} all-reduce(f32[16,2]{0,1:T(2,128)S(1)} %convolution_bitcast_fusion.5), channel_id=1, replica_groups=mesh['gx'=16,'gy'=4,'tx'=4] {'gx','gy'}, use_global_device_ids=true, to_apply=%region_21.25 | all-reduce | flops 32 | bytes 256 | tf_op jit(solution)/shard_map/psum | solution.py:141
  1603.7 3.3 multiply_reduce_fusion.4
  1607.0 138.7 %psum.123 = f32[1,2]{1,0:T(1,128)S(1)} all-reduce(f32[1,2]{1,0:T(1,128)S(1)} %bitcast.338), channel_id=1, replica_groups=mesh['gx'=16,'gy'=4,'tx'=4] {'gx','gy'}, use_global_device_ids=true, to_apply=%region_23.27 | all-reduce | flops 2 | bytes 16 | tf_op jit(solution)/shard_map/psum | solution.py:144
  1746.3 140.5 %psum.124 = f32[2]{0:T(128)S(1)} all-reduce(f32[2]{0:T(128)S(1)} %get-tuple-element.43), channel_id=1, replica_groups=mesh['gx'=16,'gy'=4,'tx'=4] {'gx','gy'}, use_global_device_ids=true, to_apply=%region_25.29 | all-reduce | flops 2 | bytes 16 | tf_op jit(solution)/shard_map/psum | solution.py:147
  1889.0 5.8 collective-permute-start.13
  1899.2 3.9 collective-permute-start.15
  1903.2 4.9 collective-permute-done.14
  1910.0 2.4 select_maximum_fusion
  1920.0 3.7 convolution_bitcast_fusion.4
  1923.7 140.9 %psum.125 = f32[16,2]{0,1:T(2,128)S(1)} all-reduce(f32[16,2]{0,1:T(2,128)S(1)} %convolution_bitcast_fusion.4), channel_id=1, replica_groups=mesh['gx'=16,'gy'=4,'tx'=4] {'gx','gy'}, use_global_device_ids=true, to_apply=%region_26.30 | all-reduce | flops 32 | bytes 256 | tf_op jit(solution)/shard_map/psum | solution.py:141
  2064.9 3.4 multiply_reduce_fusion.2
  2068.3 139.0 %psum.126 = f32[2,2]{1,0:T(2,128)S(1)} all-reduce(f32[2,2]{1,0:T(2,128)S(1)} %pad_maximum_fusion.27), channel_id=1, replica_groups=mesh['gx'=16,'gy'=4,'tx'=4] {'gx','gy'}, use_global_device_ids=true, to_apply=%region_29.33 | all-reduce | flops 4 | bytes 32 | tf_op jit(solution)/shard_map/psum | solution.py:144
  2208.7 140.2 %psum.127 = f32[2]{0:T(128)S(1)} all-reduce(f32[2]{0:T(128)S(1)} %get-tuple-element.41), channel_id=1, replica_groups=mesh['gx'=16,'gy'=4,'tx'=4] {'gx','gy'}, use_global_device_ids=true, to_apply=%region_31.35 | all-reduce | flops 2 | bytes 16 | tf_op jit(solution)/shard_map/psum | solution.py:147
  2353.7 2.7 fusion
  (225 shorter events, 80.5 us)
Async XLA Ops:
  7.2 46.0 %all-gather.3.cloned.1.call-start = ((), (), s32[]{:S(2)}) async-start(), calls=%async_computation | async-start | bytes 1966080 | tf_op jit(solution)/shard_map/all_gather | solution.py:113
  7.9 1422.9 %all-gather.5.cloned.1.call-start = ((), (), s32[]{:S(2)}) async-start(), calls=%async_computation.1 | async-start | bytes 1966080 | tf_op jit(solution)/shard_map/all_gather | solution.py:112
  53.1 5.4 copy-start.1
  358.2 7.7 collective-permute-start
  360.2 7.5 collective-permute-start.1
  368.5 10.8 collective-permute-start.2
  370.4 10.8 collective-permute-start.3
  389.8 1.4 copy-start.2
  819.5 7.8 collective-permute-start.4
  821.4 7.5 collective-permute-start.5
  829.7 10.8 collective-permute-start.6
  831.6 10.8 collective-permute-start.7
  851.0 1.4 copy-start.3
  1423.1 11.5 collective-permute-start.8
  1425.0 9.5 collective-permute-start.9
  1435.4 11.7 collective-permute-start.10
  1437.3 11.7 collective-permute-start.11
  1457.6 1.4 copy-start.4
  1887.0 7.8 collective-permute-start.12
  1889.0 7.5 collective-permute-start.13
  1897.3 10.8 collective-permute-start.14
  1899.2 10.8 collective-permute-start.15
  1918.6 1.4 copy-start.5
  2349.7 4.0 copy-start
Sparse Core Ops, SparseCore 0:
  9.8 43.2 all-gather.2
  366.1 35.2 all-gather.4
where the time goes:
time: 2380 us; the launch traced here: 2370 us
  blocking collectives  2120 us (89%)
  waiting for transfers between devices  59.9 us (3%)
  starting transfers between devices  54.6 us (2%)
  matrix products  50.6 us (2%)
  other arithmetic  50.3 us (2%)
    psum x4, blocking collectives, on_device(): g_raw = lax.psum(inner_basis(all_images, work), ('gx', 'gy'))  564 us
    psum x4, blocking collectives, on_device(): h_next = jnp.sqrt(lax.psum(per_source(work, work), ('gx', 'gy')) + eps)  560 us
    psum x4, blocking collectives, on_device(): lax.psum(jnp.stack([per_source(vec, work) for vec in krylov]), ('gx', 'gy'))  556 us
    psum x2, blocking collectives, on_device(): lax.psum(per_source(residual, residual), ('gx', 'gy')) + eps  283 us
    psum x1, blocking collectives, on_device(): lax.psum((gram_part, inner_basis(all_images, rhs)), ('gx', 'gy'))  144 us
  transfers between devices with their start and end apart: 18, of which 12 were waited for; matrix products, arithmetic and copies ran while one was open for 2% of the time, Pallas kernels for 0%

commit v1 on v0

--- a/solution.py
+++ b/solution.py
@@ -126,7 +126,7 @@
     gram_part = jnp.einsum(
         "kpczxy,lpczxy->kl", all_images, all_images, preferred_element_type=jnp.float32
     )
-    gram, start_inner = lax.psum((gram_part, inner_basis(all_images, rhs)), ("gx", "gy"))
+    gram, start_inner = lax.psum(lax.psum((gram_part, inner_basis(all_images, rhs)), "gx"), "gy")
     factor = jnp.linalg.cholesky(gram)
     h_zero = jax.scipy.linalg.cho_solve((factor, True), start_inner)
     residual = rhs - combine(h_zero, all_images)

time: 2380 us -> 2270 us (0.954)
  blocking collectives: 2120 us -> 2020 us
    psum x1 -> x2, blocking collectives: 144 us -> 41.3 us  [the longest x1 32.5 us: on_device(): lax.psum((gram_part, inner_basis(all_images, rhs)), 'gx')]
where the time goes in v1:
time: 2270 us; the launch traced here: 2260 us
  blocking collectives  2020 us (89%)
  waiting for transfers between devices  59.9 us (3%)
  starting transfers between devices  54.6 us (2%)
  matrix products  50.6 us (2%)
  other arithmetic  50.3 us (2%)
    psum x4, blocking collectives, on_device(): g_raw = lax.psum(inner_basis(all_images, work), ('gx', 'gy'))  564 us
    psum x4, blocking collectives, on_device(): h_next = jnp.sqrt(lax.psum(per_source(work, work), ('gx', 'gy')) + eps)  560 us
    psum x4, blocking collectives, on_device(): lax.psum(jnp.stack([per_source(vec, work) for vec in krylov]), ('gx', 'gy'))  556 us
    psum x2, blocking collectives, on_device(): lax.psum(per_source(residual, residual), ('gx', 'gy')) + eps  280 us
  transfers between devices with their start and end apart: 18, of which 12 were waited for; matrix products, arithmetic and copies ran while one was open for 2% of the time, Pallas kernels for 0%

profile of v1, /device:TPU:40, one launch (start us, length us, event | category | flops | bytes accessed | tf_op | source)
XLA Modules:
  0.0 2260.3 jit_solution(12238891105085259908)
XLA Ops:
  7.9 16.6 all_gather.10
  26.5 26.6 %all-gather.3.cloned.1.call-done = bf16[16,2,3,8,8,128]{5,4,3,2,1,0:T(8,128)(2,1)} async-done(((bf16[4,2,3,8,8,128]{5,4,3,2,1,0:T(8,128)(2,1)}), bf16[16,2,3,8,8,128]{5,4,3,2,1,0:T(8,128)(2,1)}) %all-gather.3.cloned.1.call-update) | async-done | bytes 1572880 | tf_op jit(solution)/shard_map/all_gather | solution.py:113
  53.1 5.4 convolution_bitcast_fusion
  58.5 3.7 convolution_bitcast_fusion.8
  62.2 32.5 %all-reduce.54 = (f32[16,2]{0,1:T(2,128)S(1)}, f32[16,16]{0,1:T(8,128)S(1)}) all-reduce(f32[16,2]{0,1:T(2,128)S(1)} %convolution_bitcast_fusion.8, f32[16,16]{0,1:T(8,128)S(1)} %convolution_bitcast_fusion), channel_id=1, replica_groups=mesh['gx'=16,'gy'=4,'tx'=4] {'gx'}, use_global_device_ids=true, to_apply=%region_4.5 | all-reduce | flops 288 | bytes 2304 | tf_op jit(solution)/shard_map/psum | solution.py:129
  94.7 8.8 all-reduce.55
  107.9 3.3 multiply_reduce_fusion.11
  111.2 141.1 %psum.130 = f32[2]{0:T(128)S(1)} all-reduce(f32[2]{0:T(128)S(1)} %get-tuple-element.121), channel_id=1, replica_groups=mesh['gx'=16,'gy'=4,'tx'=4] {'gx','gy'}, use_global_device_ids=true, to_apply=%region_7.9 | all-reduce | flops 2 | bytes 16 | tf_op jit(solution)/shard_map/psum | solution.py:135
  254.4 5.8 collective-permute-start.1
  264.7 4.1 collective-permute-start.3
  268.8 4.7 collective-permute-done.2
  273.6 1.9 collective-permute-done.3
  275.5 2.4 select_maximum_fusion.12
  285.5 3.7 convolution_bitcast_fusion.7
  289.2 140.9 %psum.131 = f32[16,2]{0,1:T(2,128)S(1)} all-reduce(f32[16,2]{0,1:T(2,128)S(1)} %convolution_bitcast_fusion.7), channel_id=1, replica_groups=mesh['gx'=16,'gy'=4,'tx'=4] {'gx','gy'}, use_global_device_ids=true, to_apply=%region_8.10 | all-reduce | flops 32 | bytes 256 | tf_op jit(solution)/shard_map/psum | solution.py:141
  430.4 3.3 multiply_reduce_fusion.10
  433.7 139.6 %psum.132 = f32[1,2]{1,0:T(1,128)S(1)} all-reduce(f32[1,2]{1,0:T(1,128)S(1)} %bitcast.337), channel_id=1, replica_groups=mesh['gx'=16,'gy'=4,'tx'=4] {'gx','gy'}, use_global_device_ids=true, to_apply=%region_10.12 | all-reduce | flops 2 | bytes 16 | tf_op jit(solution)/shard_map/psum | solution.py:144
  574.0 139.6 %psum.133 = f32[2]{0:T(128)S(1)} all-reduce(f32[2]{0:T(128)S(1)} %get-tuple-element.51), channel_id=1, replica_groups=mesh['gx'=16,'gy'=4,'tx'=4] {'gx','gy'}, use_global_device_ids=true, to_apply=%region_12.14 | all-reduce | flops 2 | bytes 16 | tf_op jit(solution)/shard_map/psum | solution.py:147
  715.7 5.8 collective-permute-start.5
  725.9 3.9 collective-permute-start.7
  729.9 4.9 collective-permute-done.6
  736.7 2.4 select_maximum_fusion.8
  746.8 3.6 convolution_bitcast_fusion.6
  750.4 141.1 %psum.134 = f32[16,2]{0,1:T(2,128)S(1)} all-reduce(f32[16,2]{0,1:T(2,128)S(1)} %convolution_bitcast_fusion.6), channel_id=1, replica_groups=mesh['gx'=16,'gy'=4,'tx'=4] {'gx','gy'}, use_global_device_ids=true, to_apply=%region_13.15 | all-reduce | flops 32 | bytes 256 | tf_op jit(solution)/shard_map/psum | solution.py:141
  891.7 3.4 multiply_reduce_fusion.8
  895.2 139.0 %psum.135 = f32[2,2]{1,0:T(2,128)S(1)} all-reduce(f32[2,2]{1,0:T(2,128)S(1)} %pad_maximum_fusion.26), channel_id=1, replica_groups=mesh['gx'=16,'gy'=4,'tx'=4] {'gx','gy'}, use_global_device_ids=true, to_apply=%region_16.18 | all-reduce | flops 4 | bytes 32 | tf_op jit(solution)/shard_map/psum | solution.py:144
  1034.9 140.2 %psum.136 = f32[2]{0:T(128)S(1)} all-reduce(f32[2]{0:T(128)S(1)} %get-tuple-element.49), channel_id=1, replica_groups=mesh['gx'=16,'gy'=4,'tx'=4] {'gx','gy'}, use_global_device_ids=true, to_apply=%region_18.20 | all-reduce | flops 2 | bytes 16 | tf_op jit(solution)/shard_map/psum | solution.py:147
  1178.1 139.0 %psum.137 = f32[2]{0:T(128)S(1)} all-reduce(f32[2]{0:T(128)S(1)} %get-tuple-element.47), channel_id=1, replica_groups=mesh['gx'=16,'gy'=4,'tx'=4] {'gx','gy'}, use_global_device_ids=true, to_apply=%region_22.26 | all-reduce | flops 2 | bytes 16 | tf_op jit(solution)/shard_map/psum | solution.py:135
  1319.3 5.8 collective-permute-start.9
  1325.1 3.7 convolution_add_fusion
  1331.6 4.1 collective-permute-start.11
  1335.8 5.5 collective-permute-done.10
  1343.3 2.4 select_maximum_fusion.4
  1353.3 3.7 convolution_bitcast_fusion.5
  1357.0 140.7 %psum.138 = f32[16,2]{0,1:T(2,128)S(1)} all-reduce(f32[16,2]{0,1:T(2,128)S(1)} %convolution_bitcast_fusion.5), channel_id=1, replica_groups=mesh['gx'=16,'gy'=4,'tx'=4] {'gx','gy'}, use_global_device_ids=true, to_apply=%region_23.27 | all-reduce | flops 32 | bytes 256 | tf_op jit(solution)/shard_map/psum | solution.py:141
  1498.0 3.3 multiply_reduce_fusion.4
  1501.3 138.7 %psum.139 = f32[1,2]{1,0:T(1,128)S(1)} all-reduce(f32[1,2]{1,0:T(1,128)S(1)} %bitcast.338), channel_id=1, replica_groups=mesh['gx'=16,'gy'=4,'tx'=4] {'gx','gy'}, use_global_device_ids=true, to_apply=%region_25.29 | all-reduce | flops 2 | bytes 16 | tf_op jit(solution)/shard_map/psum | solution.py:144
  1640.6 140.5 %psum.140 = f32[2]{0:T(128)S(1)} all-reduce(f32[2]{0:T(128)S(1)} %get-tuple-element.45), channel_id=1, replica_groups=mesh['gx'=16,'gy'=4,'tx'=4] {'gx','gy'}, use_global_device_ids=true, to_apply=%region_27.31 | all-reduce | flops 2 | bytes 16 | tf_op jit(solution)/shard_map/psum | solution.py:147
  1783.3 5.8 collective-permute-start.13
  1793.5 3.9 collective-permute-start.15
  1797.5 4.9 collective-permute-done.14
  1804.3 2.4 select_maximum_fusion
  1814.3 3.7 convolution_bitcast_fusion.4
  1818.0 140.9 %psum.141 = f32[16,2]{0,1:T(2,128)S(1)} all-reduce(f32[16,2]{0,1:T(2,128)S(1)} %convolution_bitcast_fusion.4), channel_id=1, replica_groups=mesh['gx'=16,'gy'=4,'tx'=4] {'gx','gy'}, use_global_device_ids=true, to_apply=%region_28.32 | all-reduce | flops 32 | bytes 256 | tf_op jit(solution)/shard_map/psum | solution.py:141
  1959.2 3.4 multiply_reduce_fusion.2
  1962.6 139.0 %psum.142 = f32[2,2]{1,0:T(2,128)S(1)} all-reduce(f32[2,2]{1,0:T(2,128)S(1)} %pad_maximum_fusion.27), channel_id=1, replica_groups=mesh['gx'=16,'gy'=4,'tx'=4] {'gx','gy'}, use_global_device_ids=true, to_apply=%region_31.35 | all-reduce | flops 4 | bytes 32 | tf_op jit(solution)/shard_map/psum | solution.py:144
  2103.0 140.2 %psum.143 = f32[2]{0:T(128)S(1)} all-reduce(f32[2]{0:T(128)S(1)} %get-tuple-element.43), channel_id=1, replica_groups=mesh['gx'=16,'gy'=4,'tx'=4] {'gx','gy'}, use_global_device_ids=true, to_apply=%region_33.37 | all-reduce | flops 2 | bytes 16 | tf_op jit(solution)/shard_map/psum | solution.py:147
  2248.0 2.7 fusion
  (226 shorter events, 82.4 us)
Async XLA Ops:
  7.2 46.0 %all-gather.3.cloned.1.call-start = ((), (), s32[]{:S(2)}) async-start(), calls=%async_computation | async-start | bytes 1966080 | tf_op jit(solution)/shard_map/all_gather | solution.py:113
  7.9 1317.2 %all-gather.5.cloned.1.call-start = ((), (), s32[]{:S(2)}) async-start(), calls=%async_computation.1 | async-start | bytes 1966080 | tf_op jit(solution)/shard_map/all_gather | solution.py:112
  53.1 5.4 copy-start.1
  252.5 7.7 collective-permute-start
  254.4 7.5 collective-permute-start.1
  262.8 10.8 collective-permute-start.2
  264.7 10.8 collective-permute-start.3
  284.1 1.4 copy-start.2
  713.8 7.8 collective-permute-start.4
  715.7 7.5 collective-permute-start.5
  724.0 10.8 collective-permute-start.6
  725.9 10.8 collective-permute-start.7
  745.3 1.4 copy-start.3
  1317.4 11.5 collective-permute-start.8
  1319.3 9.5 collective-permute-start.9
  1329.7 11.7 collective-permute-start.10
  1331.6 11.7 collective-permute-start.11
  1351.9 1.4 copy-start.4
  1781.3 7.8 collective-permute-start.12
  1783.3 7.5 collective-permute-start.13
  1791.6 10.8 collective-permute-start.14
  1793.5 10.8 collective-permute-start.15
  1812.9 1.4 copy-start.5
  2244.0 4.0 copy-start
Sparse Core Ops, SparseCore 0:
  9.8 43.2 all-gather.2
  260.4 35.2 all-gather.4
